TPU v7x, 256 devices: a whole 4x4x8 slice. The times are simulated.
256 devices in a mesh: ctx: 32 (over z, y), head: 8 (over x, core).
Axes of the slice: x: 4, y: 4, z: 8, core: 2. Of those that a mesh axis runs over, the one named last changes fastest.
Arguments:
- query: bfloat16 [8192, 8192], P(('ctx', 'head')), may hold values from -64 to 64
- key: bfloat16 [8192, 1024], P(('ctx', 'head')), may hold values from -6 to 6
- value: bfloat16 [8192, 1024], P(('ctx', 'head')), may hold values from -6 to 6
- grad_out: bfloat16 [8192, 8192], P('ctx', 'head'), may hold values from -6 to 6
- doc_ids: int32 [64], replicated, may hold values from 0 to 5, never falling along the last dimension, each value on 1 to 16 neighbouring positions
- relay_mask: int32 [2], replicated, may hold values from 0 to 31
- drop_bits: int32 [64, 128, 4], P('head'), may hold values from -2147483648 to 2147483647
Outputs:
- out: bfloat16 [8192, 8192], P('ctx', 'head')
- grad_query: bfloat16 [8192, 8192], P(('ctx', 'head'))
- grad_key: bfloat16 [8192, 1024], P(('ctx', 'head'))
- grad_value: bfloat16 [8192, 1024], P(('ctx', 'head'))
Inputs may be any that keep to these rules, and one draw needn't show every extreme that they name: `doc_ids`: numbers never fall; each document spans 1 to 16 blocks and one spans exactly 16.
All inputs are finite; a program needn't handle non-finite values.
Results may differ from a plain program's by a relative error of at most 0.033.
Values may be sent and summed in bfloat16 or wider, within the bound.
A program may use at most 64 MiB of HBM per device.

v0:
```python
import math

import jax
import jax.numpy as jnp
from jax import lax
from jax.experimental import pallas as pl
from jax.experimental.pallas import tpu as pltpu
from jax.sharding import PartitionSpec as P

E = 128
BLK = 128
GROUP = 8
PAIRS = 8
WIN = 18 * BLK
NZ, NY, NH = 8, 4, 8
F32 = jnp.float32
BF16 = jnp.bfloat16
MESH = pl.DeviceIdType.MESH


def place():
    ctx, head = lax.axis_index("ctx"), lax.axis_index("head")
    return ctx // NY, ctx % NY, head


def remote(src, dst, send, recv, ctx, head):
    return pltpu.make_async_remote_copy(
        src_ref=src, dst_ref=dst, send_sem=send, recv_sem=recv,
        device_id=(ctx, head), device_id_type=MESH)


def greet(zi, yi, head):
    barrier = pltpu.get_barrier_semaphore()
    peers = [(zi * NY + yi, (head + d) % NH) for d in range(1, NH)]
    peers += [(((zi + d) % NZ) * NY + yi, head) for d in (1, 2, NZ - 1, NZ - 2)]
    peers += [(zi * NY + (yi + k) % NY, head) for k in range(1, NY)]
    for peer in peers:
        pl.semaphore_signal(barrier, inc=1, device_id=peer, device_id_type=MESH)
    pl.semaphore_wait(barrier, len(peers))


def ring_routes(count, rounds):
    tables = []
    for mask in range(count):
        flows = []
        for place in range(count):
            up = (place ^ mask) - place
            up %= count
            for piece in range(2):
                if up == 0:
                    continue
                down = count - up
                forward = up < down or (up == down and piece == 0)
                flows.append(dict(at=place, left=min(up, down), step=1 if forward else -1,
                                  slot=piece, piece=piece, goal=place ^ mask))
        sends = [[[0, 0] for _ in range(rounds)] for _ in range(count)]
        final = [[0, 1] for _ in range(count)]
        for t in range(rounds):
            moved = {}
            for flow in sorted(flows, key=lambda f: (-f["left"], f["piece"], f["at"])):
                if flow["left"] == 0:
                    continue
                way = 0 if flow["step"] == 1 else 1
                if (flow["at"], way) in moved:
                    continue
                moved[flow["at"], way] = flow
            for (at, way), flow in moved.items():
                sends[at][t][way] = flow["slot"]
                flow["at"] = (at + flow["step"]) % count
                flow["left"] -= 1
                flow["slot"] = 2 + 2 * t + way
                if flow["left"] == 0:
                    assert flow["at"] == flow["goal"]
                    final[flow["at"]][flow["piece"]] = flow["slot"]
        assert all(flow["left"] == 0 for flow in flows), (count, mask)
        for place in range(count):
            tables.append([s for pair in sends[place] for s in pair] + final[place])
    return tables

ZT, YT = 4, 2
Z_ROUTES = ring_routes(NZ, ZT)
Y_ROUTES = ring_routes(NY, YT)
Z_WIDE, Y_WIDE = 2 * ZT + 2, 2 * YT + 2
HALF = BLK // 2


def route_table():
    return jnp.array([v for row in Z_ROUTES + Y_ROUTES for v in row], jnp.int32)


def relay_scratch():
    half = (HALF, GROUP * E)
    dma = pltpu.SemaphoreType.DMA
    return ([pltpu.VMEM((2, ZT, 2) + half, BF16), pltpu.VMEM((2, YT, 2) + half, BF16)]
            + [pltpu.VMEM(half, BF16) for _ in range(2 * 2 * (ZT + YT))]
            + [pltpu.VMEM((2, 2) + half, BF16),
               dma((2, ZT, 2)), dma((2, ZT, 2)), dma((2, YT, 2)), dma((2, YT, 2))])


RELAY_COUNT = 2 + 2 * 2 * (ZT + YT) + 5


class Relay:
    def __init__(self, mask_ref, table_ref, src_ref, dst_ref, scratch, place_of):
        zi, yi, head = place_of
        self.src, self.dst = src_ref, dst_ref
        z_stage, y_stage = scratch[0], scratch[1]
        landing = scratch[2:-5]
        self.mid = scratch[-5]
        zs, zr, ys, yr = scratch[-4:]
        self.copies = []
        self.rings = []
        for r in range(2):
            mask = mask_ref[r]
            z_base = ((mask // NY) * NZ + zi) * Z_WIDE
            y_base = NZ * NZ * Z_WIDE + ((mask % NY) * NY + yi) * Y_WIDE
            low = r * 2 * (ZT + YT)
            z_ring = dict(
                rounds=ZT, stage=z_stage, land=landing[low:low + 2 * ZT], routes=Z_ROUTES,
                pick=[table_ref[z_base + i] for i in range(Z_WIDE)], send=zs, recv=zr,
                to=[(((zi + step) % NZ) * NY + yi, head) for step in (1, NZ - 1)])
            y_ring = dict(
                rounds=YT, stage=y_stage, land=landing[low + 2 * ZT:low + 2 * (ZT + YT)], routes=Y_ROUTES,
                pick=[table_ref[y_base + i] for i in range(Y_WIDE)], send=ys, recv=yr,
                to=[(zi * NY + (yi + step) % NY, head) for step in (1, NY - 1)])
            self.rings.append([z_ring, y_ring] if r == 0 else [y_ring, z_ring])
        self.plan = []
        for r in range(2):
            steps = []
            for which, ring in enumerate(self.rings[r]):
                steps += [(which, t) for t in range(ring["rounds"])]
            self.plan.append(steps)

    def value(self, r, which, slot):
        ring = self.rings[r][which]
        if slot >= 2:
            return ring["land"][slot - 2][...]
        if which == 0:
            return self.src[pl.ds(r * BLK + slot * HALF, HALF), :]
        return self.mid[r, slot]

    def choose(self, r, which, index):
        ring = self.rings[r][which]
        slots = sorted({row[index] for row in ring["routes"]})
        chosen = self.value(r, which, slots[0])
        for slot in slots[1:]:
            chosen = jnp.where(ring["pick"][index] == slot, self.value(r, which, slot), chosen)
        return chosen

    def settle(self, r, which):
        ring = self.rings[r][which]
        for copy in ring["last"]:
            copy.wait_recv()

    def close(self, r, which):
        self.settle(r, which)
        ring = self.rings[r][which]
        for piece in range(2):
            chosen = self.choose(r, which, 2 * ring["rounds"] + piece)
            if which == 0:
                self.mid[r, piece] = chosen
            else:
                self.dst[pl.ds(r * BLK + piece * HALF, HALF), :] = chosen

    def step(self, n):
        for r in range(2):
            which, t = self.plan[r][n]
            ring = self.rings[r][which]
            if t > 0:
                self.settle(r, which)
            elif which == 1:
                self.close(r, 0)
            ring["last"] = []
            for way in range(2):
                ring["stage"][r, t, way] = self.choose(r, which, 2 * t + way)
            for way in range(2):
                copy = remote(ring["stage"].at[r, t, way], ring["land"][2 * t + way],
                              ring["send"].at[r, t, way], ring["recv"].at[r, t, way], *ring["to"][way])
                copy.start()
                ring["last"].append(copy)
                self.copies.append(copy)

    def finish(self):
        for r in range(2):
            self.close(r, 1)

    def drain(self):
        for copy in self.copies:
            copy.wait_send()


def build_keep(bits_ref, keep_ref):
    row = lax.broadcasted_iota(jnp.int32, (32, BLK), 0)
    for h in range(GROUP):
        parts = []
        for w in range(4):
            words = jnp.broadcast_to(bits_ref[h, w:w + 1, :], (32, BLK))
            parts.append((lax.shift_right_logical(words, row) & 1).astype(F32))
        kept = jnp.concatenate(parts, axis=0).T
        keep_ref[h, 0:BLK] = kept
        keep_ref[h, BLK:2 * BLK] = kept


def gather_kernel(mask_ref, table_ref, q_ref, k_ref, v_ref, g_ref, bits_ref, qb_ref, win_ref, gb_ref, keep_ref,
                  kv_send, kv_recv, q_send, q_recv, z_send, z_recv, y_send, y_recv, own_sem, *scratch):
    zi, yi, head = place()
    ctx = zi * NY + yi
    move = Relay(mask_ref, table_ref, g_ref, gb_ref, scratch, (zi, yi, head))
    greet(zi, yi, head)
    mine = pl.ds(pl.multiple_of(head * 32, 32), 32)
    own = [
        pltpu.make_async_copy(k_ref.at[:, pl.ds(pl.multiple_of(head * E, E), E)],
                              win_ref.at[8, mine, pl.ds(0, E)], own_sem.at[0]),
        pltpu.make_async_copy(v_ref.at[:, pl.ds(pl.multiple_of(head * E, E), E)],
                              win_ref.at[8, mine, pl.ds(E, E)], own_sem.at[1]),
        pltpu.make_async_copy(q_ref.at[:, pl.ds(pl.multiple_of(head * GROUP * E, GROUP * E), GROUP * E)],
                              qb_ref.at[mine, :], own_sem.at[2]),
    ]
    for copy in own:
        copy.start()
    kv_copies = []
    for d in range(1, NH):
        to = (head + d) % NH
        cols = pl.ds(pl.multiple_of(to * E, E), E)
        for part, ref in enumerate((k_ref, v_ref)):
            copy = remote(ref.at[:, cols], win_ref.at[8, mine, pl.ds(part * E, E)],
                          kv_send.at[part, d], kv_recv.at[part, d], ctx, to)
            copy.start()
            kv_copies.append(copy)
    q_copies = []
    for d in range(1, NH):
        to = (head + d) % NH
        cols = pl.ds(pl.multiple_of(to * GROUP * E, GROUP * E), GROUP * E)
        copy = remote(q_ref.at[:, cols], qb_ref.at[mine, :], q_send.at[d], q_recv.at[d], ctx, to)
        copy.start()
        q_copies.append(copy)
    move.step(0)
    build_keep(bits_ref, keep_ref)
    own[0].wait()
    own[1].wait()
    for copy in kv_copies:
        copy.wait_recv()
    z_copies = []
    for d in (1, 2):
        copy = remote(win_ref.at[8], win_ref.at[8 - 4 * d], z_send.at[d], z_recv.at[d],
                      ((zi + d) % NZ) * NY + yi, head)
        copy.start()
        z_copies.append(copy)
    y_copies = []
    for part in range(2):
        for k in range(1, NY):
            wrap = (yi + k) // NY
            y_copies.append((part, k, wrap, remote(
                win_ref.at[8 - 4 * part - 4 * wrap], win_ref.at[8 - 4 * part - k],
                y_send.at[part, k], y_recv.at[part, k], zi * NY + (yi + k) % NY, head)))
    for part, k, wrap, copy in y_copies:
        if part == 0:
            @pl.when(wrap == 0)
            def _(copy=copy):
                copy.start()
    move.step(1)
    z_copies[0].wait_recv()
    for part, k, wrap, copy in y_copies:
        @pl.when(wrap == 1 - part)
        def _(copy=copy):
            copy.start()
    move.step(2)
    z_copies[1].wait_recv()
    for part, k, wrap, copy in y_copies:
        if part == 1:
            @pl.when(wrap == 1)
            def _(copy=copy):
                copy.start()
    for n in range(3, ZT + YT):
        move.step(n)
    move.finish()
    for copy in q_copies:
        copy.wait_recv()
    for _, _, _, copy in y_copies:
        copy.wait_recv()
    own[2].wait()
    move.drain()
    for copy in kv_copies + q_copies + z_copies:
        copy.wait_send()
    for _, _, _, copy in y_copies:
        copy.wait_send()


def gather_inputs(relay_mask, table, query, key, value, grads, bits):
    vm = pl.BlockSpec(memory_space=pltpu.VMEM)
    sm = pl.BlockSpec(memory_space=pltpu.SMEM)
    dma = pltpu.SemaphoreType.DMA
    return pl.pallas_call(
        gather_kernel,
        out_shape=(jax.ShapeDtypeStruct((2 * BLK, GROUP * E), BF16),
                   jax.ShapeDtypeStruct((9, 2 * BLK, 2 * E), BF16),
                   jax.ShapeDtypeStruct((2 * BLK, GROUP * E), BF16),
                   jax.ShapeDtypeStruct((GROUP, 2 * BLK, BLK), F32)),
        in_specs=[sm, sm, vm, vm, vm, vm, vm],
        out_specs=(vm, vm, vm, vm),
        scratch_shapes=[dma((2, NH)), dma((2, NH)), dma((NH,)), dma((NH,)), dma((3,)), dma((3,)),
                        dma((2, NY)), dma((2, NY)), dma((3,))] + relay_scratch(),
        compiler_params=pltpu.CompilerParams(collective_id=0, has_side_effects=True),
    )(relay_mask, table, query, key, value, grads, bits)


def scatter_kernel(mask_ref, table_ref, out_ref, dkv_ref, dq_ref, ob_ref, gq_ref, gk_ref, gv_ref,
                   r_ref, zs_ref, zr_ref, own_ref, fin_ref,
                   q_send, q_recv, y_send, y_recv, z_send, z_recv, kv_send, kv_recv, own_sem, *scratch):
    zi, yi, head = place()
    ctx = zi * NY + yi
    move = Relay(mask_ref, table_ref, out_ref, ob_ref, scratch, (zi, yi, head))
    greet(zi, yi, head)
    wide = pl.ds(pl.multiple_of(head * GROUP * E, GROUP * E), GROUP * E)
    slim = pl.ds(pl.multiple_of(head * E, E), E)
    y_copies = []
    for part in (1, 0):
        for k in range(1, NY):
            copy = remote(dkv_ref.at[8 - 4 * part - k], r_ref.at[part, k - 1],
                          y_send.at[part, k], y_recv.at[part, k],
                          zi * NY + (yi + NY - k) % NY, head)
            copy.start()
            y_copies.append(copy)
    move.step(0)
    q_copies = []
    for d in range(1, NH):
        to = (head + d) % NH
        rows = pl.ds(pl.multiple_of(to * 32, 32), 32)
        copy = remote(dq_ref.at[rows, :], gq_ref.at[:, wide], q_send.at[d], q_recv.at[d], ctx, to)
        copy.start()
        q_copies.append(copy)
    mine = pl.ds(pl.multiple_of(head * 32, 32), 32)
    own = [pltpu.make_async_copy(dq_ref.at[mine, :], gq_ref.at[:, wide], own_sem.at[0])]
    own[0].start()
    move.step(1)
    for copy in y_copies:
        copy.wait_recv()
    sums = [dkv_ref[8 - 4 * p].astype(F32) for p in range(3)]
    for k in range(1, NY):
        wraps = (yi + k) // NY > 0
        first, second = r_ref[0, k - 1].astype(F32), r_ref[1, k - 1].astype(F32)
        zero = jnp.zeros_like(first)
        sums[0] = sums[0] + jnp.where(wraps, zero, first)
        sums[1] = sums[1] + jnp.where(wraps, first, second)
        sums[2] = sums[2] + jnp.where(wraps, second, zero)
    zs_ref[0] = sums[1].astype(BF16)
    zs_ref[1] = sums[2].astype(BF16)
    own_ref[...] = sums[0]
    z_copies = []
    for d in (1, 2):
        copy = remote(zs_ref.at[d - 1], zr_ref.at[d - 1], z_send.at[d], z_recv.at[d],
                      ((zi + NZ - d) % NZ) * NY + yi, head)
        copy.start()
        z_copies.append(copy)
    move.step(2)
    move.step(3)
    for copy in z_copies:
        copy.wait_recv()
    fin_ref[...] = (own_ref[...] + zr_ref[0].astype(F32) + zr_ref[1].astype(F32)).astype(BF16)
    kv_copies = []
    for d in range(1, NH):
        to = (head + d) % NH
        rows = pl.ds(pl.multiple_of(to * 32, 32), 32)
        for part, ref in enumerate((gk_ref, gv_ref)):
            copy = remote(fin_ref.at[rows, pl.ds(part * E, E)], ref.at[:, slim],
                          kv_send.at[part, d], kv_recv.at[part, d], ctx, to)
            copy.start()
            kv_copies.append(copy)
    for part, ref in enumerate((gk_ref, gv_ref)):
        copy = pltpu.make_async_copy(fin_ref.at[mine, pl.ds(part * E, E)], ref.at[:, slim],
                                     own_sem.at[1 + part])
        copy.start()
        own.append(copy)
    move.step(4)
    move.step(5)
    move.finish()
    for copy in q_copies + kv_copies:
        copy.wait_recv()
    for copy in own:
        copy.wait()
    move.drain()
    for copy in q_copies + kv_copies + y_copies + z_copies:
        copy.wait_send()


def scatter_grads(relay_mask, table, out, dkv, dq):
    vm = pl.BlockSpec(memory_space=pltpu.VMEM)
    sm = pl.BlockSpec(memory_space=pltpu.SMEM)
    dma = pltpu.SemaphoreType.DMA
    return pl.pallas_call(
        scatter_kernel,
        out_shape=(jax.ShapeDtypeStruct((2 * BLK, GROUP * E), BF16),
                   jax.ShapeDtypeStruct((32, NH * GROUP * E), BF16),
                   jax.ShapeDtypeStruct((32, NH * E), BF16),
                   jax.ShapeDtypeStruct((32, NH * E), BF16)),
        in_specs=[sm, sm, vm, vm, vm],
        out_specs=(vm, vm, vm, vm),
        scratch_shapes=[
            pltpu.VMEM((2, NY - 1, 2 * BLK, 2 * E), BF16),
            pltpu.VMEM((2, 2 * BLK, 2 * E), BF16),
            pltpu.VMEM((2, 2 * BLK, 2 * E), BF16),
            pltpu.VMEM((2 * BLK, 2 * E), F32),
            pltpu.VMEM((2 * BLK, 2 * E), BF16),
            dma((NH,)), dma((NH,)), dma((2, NY)), dma((2, NY)), dma((3,)), dma((3,)),
            dma((2, NH)), dma((2, NH)), dma((3,))] + relay_scratch(),
        compiler_params=pltpu.CompilerParams(collective_id=1, has_side_effects=True),
    )(relay_mask, table, out, dkv, dq)


def dot_nt(a, b):
    return lax.dot_general(a, b, (((1,), (1,)), ((), ())), preferred_element_type=F32)


def dot_nn(a, b):
    return lax.dot_general(a, b, (((1,), (0,)), ((), ())), preferred_element_type=F32)


def attn_kernel(docs_ref, q_ref, kv_ref, g_ref, keep_ref, out_ref, dq_ref, dkv_ref,
                s_ref, w_ref, qs_ref, gs_ref, qt_ref, gt_ref, acc_ref, mx_ref,
                dkt_ref, dvt_ref, st_ref):
    root = 1.0 / math.sqrt(E)
    expo = root * math.log2(math.e)
    scale = 1.0 / 0.9
    lane = lax.broadcasted_iota(jnp.int32, (BLK, BLK), 1)
    row = lax.broadcasted_iota(jnp.int32, (BLK, BLK), 0)
    dkt_ref[...] = jnp.zeros_like(dkt_ref)
    dvt_ref[...] = jnp.zeros_like(dvt_ref)
    first_abs = 2 * lax.axis_index("ctx") - 16
    causal = jnp.where(lane <= row, 0.0, -jnp.inf).astype(F32)
    lane2 = lax.broadcasted_iota(jnp.int32, (1, 2 * BLK), 1)

    for r in range(2):
        document = docs_ref[first_abs + 16 + r]
        low = 16 + r
        for w in range(1 + r, 16 + r):
            there = jnp.maximum(first_abs + w, 0)
            same = (docs_ref[there] == document) & (first_abs + w >= 0)
            low = low - same.astype(jnp.int32)
        start = (low - (1 + r)) // 2
        rows = pl.ds(r * BLK, BLK)
        for h in range(GROUP):
            cols = pl.ds(h * E, E)
            part = q_ref[rows, cols]
            qs_ref[pl.ds(h * BLK, BLK), :] = part
            qt_ref[:, pl.ds(h * BLK, BLK)] = part.T
        mx_ref[...] = jnp.full_like(mx_ref, -jnp.inf)

        def window(j):
            return pl.ds(pl.multiple_of((1 + r) * BLK + j * 2 * BLK, BLK), 2 * BLK)

        def score_step(j, extra, r=r, low=low):
            s = dot_nt(qs_ref[...], kv_ref[window(j), 0:E])
            block = (1 + r) + 2 * j + lane2 // BLK
            bias = jnp.where(block >= low, 0.0, -jnp.inf).astype(F32)
            for h in range(GROUP):
                part = s[h * BLK:(h + 1) * BLK] + bias
                left, right = part[:, :BLK], part[:, BLK:]
                if extra:
                    right = right + causal
                hr = pl.ds(h * BLK, BLK)
                s_ref[j, hr, 0:BLK] = left
                s_ref[j, hr, BLK:2 * BLK] = right
                mx_ref[hr, :] = jnp.maximum(mx_ref[hr, :], jnp.maximum(left, right))

        def score_body(j, c):
            score_step(j, False)
            return c
        lax.fori_loop(start, PAIRS - 1, score_body, 0)
        score_step(PAIRS - 1, True)

        for h in range(GROUP):
            hr = pl.ds(h * BLK, BLK)
            top = jnp.max(mx_ref[hr, :], axis=1, keepdims=True)
            st_ref[hr, :] = jnp.broadcast_to(top, (BLK, BLK))
        mx_ref[...] = jnp.zeros_like(mx_ref)
        acc_ref[...] = jnp.zeros_like(acc_ref)

        def out_body(j, c, r=r):
            kb = first_abs + (1 + r) + 2 * j
            kb = jnp.where(kb < 0, BLK - 1, kb)
            for h in range(GROUP):
                hr = pl.ds(h * BLK, BLK)
                top = st_ref[hr, :]
                left = jnp.exp2((s_ref[j, hr, 0:BLK] - top) * expo)
                right = jnp.exp2((s_ref[j, hr, BLK:2 * BLK] - top) * expo)
                s_ref[j, hr, 0:BLK] = left
                s_ref[j, hr, BLK:2 * BLK] = right
                mx_ref[hr, :] = mx_ref[hr, :] + (left + right)
                w_ref[j, hr, 0:BLK] = (left * keep_ref[h, pl.ds(kb, BLK), :]).astype(BF16)
                w_ref[j, hr, BLK:2 * BLK] = (right * keep_ref[h, pl.ds(kb + 1, BLK), :]).astype(BF16)
            acc_ref[...] += dot_nn(w_ref[j], kv_ref[window(j), E:2 * E])
            return c
        lax.fori_loop(start, PAIRS, out_body, 0)

        for h in range(GROUP):
            hr = pl.ds(h * BLK, BLK)
            cols = pl.ds(h * E, E)
            total = jnp.sum(mx_ref[hr, :], axis=1, keepdims=True)
            inverse = 1.0 / total
            o = (acc_ref[hr, :] * (inverse * scale)).astype(BF16)
            out_ref[rows, cols] = o
            grad = g_ref[rows, cols].astype(F32)
            delta = jnp.sum(grad * o.astype(F32), axis=1, keepdims=True) * inverse
            st_ref[hr, :] = jnp.broadcast_to(delta, (BLK, BLK))
            scaled = (grad * (inverse * scale)).astype(BF16)
            gs_ref[hr, :] = scaled
            gt_ref[:, hr] = scaled.T
        acc_ref[...] = jnp.zeros_like(acc_ref)

        def grad_body(j, c, r=r):
            kb = first_abs + (1 + r) + 2 * j
            kb = jnp.where(kb < 0, BLK - 1, kb)
            dw = dot_nt(gs_ref[...], kv_ref[window(j), E:2 * E])
            dvt_ref[:, window(j)] += dot_nn(gt_ref[...], w_ref[j])
            for h in range(GROUP):
                hr = pl.ds(h * BLK, BLK)
                delta = st_ref[hr, :]
                part = dw[h * BLK:(h + 1) * BLK]
                left = s_ref[j, hr, 0:BLK] * (part[:, :BLK] * keep_ref[h, pl.ds(kb, BLK), :] - delta)
                right = s_ref[j, hr, BLK:2 * BLK] * (part[:, BLK:] * keep_ref[h, pl.ds(kb + 1, BLK), :] - delta)
                w_ref[j, hr, 0:BLK] = left.astype(BF16)
                w_ref[j, hr, BLK:2 * BLK] = right.astype(BF16)
            acc_ref[...] += dot_nn(w_ref[j], kv_ref[window(j), 0:E])
            dkt_ref[:, window(j)] += dot_nn(qt_ref[...], w_ref[j])
            return c
        lax.fori_loop(start, PAIRS, grad_body, 0)

        for h in range(GROUP):
            hr = pl.ds(h * BLK, BLK)
            dq_ref[rows, pl.ds(h * E, E)] = (acc_ref[hr, :] * root).astype(BF16)

    for w in range(WIN // (2 * BLK)):
        cs = pl.ds(w * 2 * BLK, 2 * BLK)
        dkv_ref[cs, 0:E] = (dkt_ref[:, cs] * root).T.astype(BF16)
        dkv_ref[cs, E:2 * E] = dvt_ref[:, cs].T.astype(BF16)


def attention(docs, q, kv, g, keep):
    vm = pl.BlockSpec(memory_space=pltpu.VMEM)
    return pl.pallas_call(
        attn_kernel,
        out_shape=(jax.ShapeDtypeStruct((2 * BLK, GROUP * E), BF16),
                   jax.ShapeDtypeStruct((2 * BLK, GROUP * E), BF16),
                   jax.ShapeDtypeStruct((WIN, 2 * E), BF16)),
        in_specs=[pl.BlockSpec(memory_space=pltpu.SMEM), vm, vm, vm, vm],
        out_specs=(vm, vm, vm),
        scratch_shapes=[
            pltpu.VMEM((PAIRS, GROUP * BLK, 2 * BLK), F32),
            pltpu.VMEM((PAIRS, GROUP * BLK, 2 * BLK), BF16),
            pltpu.VMEM((GROUP * BLK, E), BF16),
            pltpu.VMEM((GROUP * BLK, E), BF16),
            pltpu.VMEM((E, GROUP * BLK), BF16),
            pltpu.VMEM((E, GROUP * BLK), BF16),
            pltpu.VMEM((GROUP * BLK, E), F32),
            pltpu.VMEM((GROUP * BLK, BLK), F32),
            pltpu.VMEM((E, WIN), F32),
            pltpu.VMEM((E, WIN), F32),
            pltpu.VMEM((GROUP * BLK, BLK), F32),
        ],
        cost_estimate=pl.CostEstimate(flops=6 * 10**9, bytes_accessed=6 * 10**6, transcendentals=4 * 10**6),
    )(docs, q, kv, g, keep)


def on_device(query, key, value, grad_out, doc_ids, relay_mask, drop_bits):
    table = route_table()
    q_local, window, grads, keep = gather_inputs(
        relay_mask, table, query, key, value, grad_out, drop_bits.transpose(0, 2, 1))
    out, dq, dkv = attention(doc_ids, q_local, window.reshape(WIN, 2 * E), grads, keep)
    return scatter_grads(relay_mask, table, out, dkv.reshape(9, 2 * BLK, 2 * E), dq)


def solution(mesh):
    placed = (
        P(("ctx", "head"), None),
        P(("ctx", "head"), None),
        P(("ctx", "head"), None),
        P("ctx", "head"),
        P(),
        P(),
        P("head", None, None),
    )
    return jax.shard_map(
        on_device,
        mesh=mesh,
        in_specs=placed,
        out_specs=(
            P("ctx", "head"),
            P(("ctx", "head"), None),
            P(("ctx", "head"), None),
            P(("ctx", "head"), None),
        ),
        check_vma=False,
    )
```

profile of v0, /device:TPU:6, one launch (start us, length us, event | category | flops | bytes accessed | tf_op | source)
XLA Modules:
  0.0 140.1 jit_solution(71885769459068239)
XLA Ops:
  0.6 52.4 %shard_map.111 = (bf16[256,1024]{1,0:T(8,128)(2,1)}, bf16[9,256,256]{2,1,0:T(8,128)(2,1)}, bf16[256,1024]{1,0:T(8,128)(2,1)}, f32[8,256,128]{2,1,0:T(8,128)}) custom-call(s32[2]{0:T(128)} %mask_ref.3, s32[736]{0:T(1024)} %constant.2.clone.table_ref, bf16[32,8192]{1,0:T(8,128)(2,1)} %q_ref.1, bf16[32,1024]{1,0:T(8,128)(2,1)} %k_ref.1, ...), custom_call_target="tpu_custom_call" | custom-call | tf_op jit(solution)/shard_map/pallas_call | solution.py:293
  53.0 8.7 %shard_map.112 = (bf16[256,1024]{1,0:T(8,128)(2,1)}, bf16[256,1024]{1,0:T(8,128)(2,1)}, bf16[2304,256]{1,0:T(8,128)(2,1)}) custom-call(s32[64]{0:T(128)} %docs_ref.1, bf16[256,1024]{1,0:T(8,128)(2,1)} %get-tuple-element.11.q_ref, bf16[2304,256]{1,0:T(8,128)(2,1)} %bitcast.5, bf16[256,1024]{1,0:T(8,128)(2,1)} %get-tuple-element.13.g_ref, ...), custom_call_target="tpu_custom_call" | custom-call | flops 6000000000 | bytes 6000000 | tf_op jit(solution)/shard_map/pallas_call | solution.py:540
  61.8 74.3 %shard_map.113 = (bf16[256,1024]{1,0:T(8,128)(2,1)}, bf16[32,8192]{1,0:T(8,128)(2,1)}, bf16[32,1024]{1,0:T(8,128)(2,1)}, bf16[32,1024]{1,0:T(8,128)(2,1)}) custom-call(s32[2]{0:T(128)} %mask_ref.3, s32[736]{0:T(1024)} %constant.2.clone.table_ref, bf16[256,1024]{1,0:T(8,128)(2,1)} %get-tuple-element.15.out_ref, bf16[9,256,256]{2,1,0:T(8,128)(2,1)} %bitcast.3, ...), custom_call_target="tpu_custom_call" | custom-call | tf_op jit(solution)/shard_map/pallas_call | solution.py:390
  136.1 0.0 copy-start
  136.1 0.0 copy-start.2
  136.1 0.0 copy-start.1
  136.1 1.9 %copy.16 = bf16[256,1024]{1,0:T(8,128)(2,1)} copy(bf16[256,1024]{1,0:T(8,128)(2,1)} %get-tuple-element.22) | data formatting | bytes 1048576
  138.1 0.0 copy-done
  138.1 0.8 copy.17
  138.9 0.0 copy-done.2
  138.9 0.6 copy.18
  139.5 0.0 copy-done.1
  139.5 0.6 copy.19
Async XLA Ops:
  136.1 2.0 %copy-start = (bf16[32,8192]{1,0:T(8,128)(2,1)S(1)}, bf16[32,8192]{1,0:T(8,128)(2,1)}, u32[]{:S(2)}) copy-start(bf16[32,8192]{1,0:T(8,128)(2,1)} %get-tuple-element.23) | copy-start | bytes 1572868
  136.1 2.7 %copy-start.2 = (bf16[32,1024]{1,0:T(8,128)(2,1)S(1)}, bf16[32,1024]{1,0:T(8,128)(2,1)}, u32[]{:S(2)}) copy-start(bf16[32,1024]{1,0:T(8,128)(2,1)} %get-tuple-element.24) | copy-start | bytes 196612
  136.1 3.4 %copy-start.1 = (bf16[32,1024]{1,0:T(8,128)(2,1)S(1)}, bf16[32,1024]{1,0:T(8,128)(2,1)}, u32[]{:S(2)}) copy-start(bf16[32,1024]{1,0:T(8,128)(2,1)} %get-tuple-element.25) | copy-start | bytes 196612
where the time goes:
time: 139 us; the launch traced here: 140 us
  Pallas kernels  135 us (97%)
  local copies, waits for them, and re-layouts  3.99 us (3%)
    pallas_call x1, Pallas kernels, scatter_grads(): pl.pallas_call(scatter_kernel, out_shape=(jax.ShapeDtypeStruct((2 * BLK,...  74.3 us
    pallas_call x1, Pallas kernels, gather_inputs(): pl.pallas_call(gather_kernel, out_shape=(jax.ShapeDtypeStruct((2 * BLK, G...  52.4 us
    pallas_call x1, Pallas kernels, attention(): pl.pallas_call(attn_kernel, out_shape=(jax.ShapeDtypeStruct((2 * BLK, GRO...  8.73 us
    unnamed x10, local copies, waits for them, and re-layouts  3.99 us

commit v1 on v0

v1 whole, which is shorter than its diff:
```python
import math

import jax
import jax.numpy as jnp
from jax import lax
from jax.experimental import pallas as pl
from jax.experimental.pallas import tpu as pltpu
from jax.sharding import PartitionSpec as P

E = 128
BLK = 128
GROUP = 8
PAIRS = 8
WIN = 18 * BLK
NZ, NY, NH = 8, 4, 8
F32 = jnp.float32
BF16 = jnp.bfloat16
MESH = pl.DeviceIdType.MESH


def place():
    ctx, head = lax.axis_index("ctx"), lax.axis_index("head")
    return ctx // NY, ctx % NY, head


def remote(src, dst, send, recv, ctx, head):
    return pltpu.make_async_remote_copy(
        src_ref=src, dst_ref=dst, send_sem=send, recv_sem=recv,
        device_id=(ctx, head), device_id_type=MESH)


def greet(zi, yi, head):
    barrier = pltpu.get_barrier_semaphore()
    peers = [(zi * NY + yi, (head + d) % NH) for d in range(1, NH)]
    peers += [(((zi + d) % NZ) * NY + yi, head) for d in (1, 2, NZ - 1, NZ - 2)]
    peers += [(zi * NY + (yi + k) % NY, head) for k in range(1, NY)]
    for peer in peers:
        pl.semaphore_signal(barrier, inc=1, device_id=peer, device_id_type=MESH)
    pl.semaphore_wait(barrier, len(peers))


def ring_routes(count, rounds):
    tables = []
    for mask in range(count):
        flows = []
        for place in range(count):
            up = (place ^ mask) - place
            up %= count
            for piece in range(2):
                if up == 0:
                    continue
                down = count - up
                forward = up < down or (up == down and piece == 0)
                flows.append(dict(at=place, left=min(up, down), step=1 if forward else -1,
                                  slot=piece, piece=piece, goal=place ^ mask))
        sends = [[[0, 0] for _ in range(rounds)] for _ in range(count)]
        final = [[0, 1] for _ in range(count)]
        for t in range(rounds):
            moved = {}
            for flow in sorted(flows, key=lambda f: (-f["left"], f["piece"], f["at"])):
                if flow["left"] == 0:
                    continue
                way = 0 if flow["step"] == 1 else 1
                if (flow["at"], way) in moved:
                    continue
                moved[flow["at"], way] = flow
            for (at, way), flow in moved.items():
                sends[at][t][way] = flow["slot"]
                flow["at"] = (at + flow["step"]) % count
                flow["left"] -= 1
                flow["slot"] = 2 + 2 * t + way
                if flow["left"] == 0:
                    assert flow["at"] == flow["goal"]
                    final[flow["at"]][flow["piece"]] = flow["slot"]
        assert all(flow["left"] == 0 for flow in flows), (count, mask)
        for place in range(count):
            tables.append([s for pair in sends[place] for s in pair] + final[place])
    return tables

ZT, YT = 4, 2
Z_ROUTES = ring_routes(NZ, ZT)
Y_ROUTES = ring_routes(NY, YT)
Z_WIDE, Y_WIDE = 2 * ZT + 2, 2 * YT + 2
STEPS = ZT + YT
HALF = BLK // 2
SPAN = GROUP * E // 2
STREAMS = ((0, 0, "zy"), (1, 0, "yz"), (0, 1, "yz"), (1, 1, "zy"))


def route_table():
    return jnp.array([v for row in Z_ROUTES + Y_ROUTES for v in row], jnp.int32)


def relay_scratch():
    count = len(STREAMS)
    dma = pltpu.SemaphoreType.DMA
    piece = (HALF, SPAN)
    return [pltpu.VMEM((count, ZT, 2) + piece, BF16), pltpu.VMEM((count, ZT, 2) + piece, BF16),
            pltpu.VMEM((count, YT, 2) + piece, BF16), pltpu.VMEM((count, YT, 2) + piece, BF16),
            pltpu.VMEM((count, 2) + piece, BF16),
            dma((count, ZT, 2)), dma((count, ZT, 2)), dma((count, YT, 2)), dma((count, YT, 2))]


RELAY_REFS = 9


class Relay:
    def __init__(self, mask_ref, table_ref, src_ref, dst_ref, scratch, place_of):
        zi, yi, head = place_of
        z_stage, z_land, y_stage, y_land, self.mid, zs, zr, ys, yr = scratch
        self.src, self.dst = src_ref, dst_ref
        self.copies = []
        self.rings = []
        self.plan = []
        for n, (r, _, order) in enumerate(STREAMS):
            mask = mask_ref[r]
            z_base = ((mask // NY) * NZ + zi) * Z_WIDE
            y_base = NZ * NZ * Z_WIDE + ((mask % NY) * NY + yi) * Y_WIDE
            rings = dict(
                z=dict(rounds=ZT, stage=z_stage, land=z_land, routes=Z_ROUTES, send=zs, recv=zr,
                       pick=[table_ref[z_base + i] for i in range(Z_WIDE)],
                       to=[(((zi + step) % NZ) * NY + yi, head) for step in (1, NZ - 1)]),
                y=dict(rounds=YT, stage=y_stage, land=y_land, routes=Y_ROUTES, send=ys, recv=yr,
                       pick=[table_ref[y_base + i] for i in range(Y_WIDE)],
                       to=[(zi * NY + (yi + step) % NY, head) for step in (1, NY - 1)]))
            self.rings.append([rings[axis] for axis in order])
            self.plan.append([(which, t) for which in range(2)
                              for t in range(self.rings[n][which]["rounds"])])

    def region(self, n, piece):
        r, part, _ = STREAMS[n]
        return pl.ds(r * BLK + piece * HALF, HALF), pl.ds(part * SPAN, SPAN)

    def value(self, n, which, slot):
        ring = self.rings[n][which]
        if slot >= 2:
            return ring["land"][n, (slot - 2) // 2, slot % 2]
        if which == 0:
            return self.src[self.region(n, slot)]
        return self.mid[n, slot]

    def choose(self, n, which, index):
        ring = self.rings[n][which]
        slots = sorted({row[index] for row in ring["routes"]})
        chosen = self.value(n, which, slots[0])
        for slot in slots[1:]:
            chosen = jnp.where(ring["pick"][index] == slot, self.value(n, which, slot), chosen)
        return chosen

    def close(self, n, which):
        ring = self.rings[n][which]
        for copy in ring["last"]:
            copy.wait_recv()
        for piece in range(2):
            chosen = self.choose(n, which, 2 * ring["rounds"] + piece)
            if which == 0:
                self.mid[n, piece] = chosen
            else:
                self.dst[self.region(n, piece)] = chosen

    def step(self, k):
        for n in range(len(STREAMS)):
            which, t = self.plan[n][k]
            ring = self.rings[n][which]
            if t > 0:
                for copy in ring["last"]:
                    copy.wait_recv()
            elif which == 1:
                self.close(n, 0)
            ring["last"] = []
            for way in range(2):
                ring["stage"][n, t, way] = self.choose(n, which, 2 * t + way)
            for way in range(2):
                copy = remote(ring["stage"].at[n, t, way], ring["land"].at[n, t, way],
                              ring["send"].at[n, t, way], ring["recv"].at[n, t, way], *ring["to"][way])
                copy.start()
                ring["last"].append(copy)
                self.copies.append(copy)

    def finish(self):
        for n in range(len(STREAMS)):
            self.close(n, 1)

    def drain(self):
        for copy in self.copies:
            copy.wait_send()


def build_keep(bits_ref, keep_ref):
    row = lax.broadcasted_iota(jnp.int32, (32, BLK), 0)
    for h in range(GROUP):
        parts = []
        for w in range(4):
            words = jnp.broadcast_to(bits_ref[h, w:w + 1, :], (32, BLK))
            parts.append((lax.shift_right_logical(words, row) & 1).astype(F32))
        kept = jnp.concatenate(parts, axis=0).T
        keep_ref[h, 0:BLK] = kept
        keep_ref[h, BLK:2 * BLK] = kept


def dot_nt(a, b):
    return lax.dot_general(a, b, (((1,), (1,)), ((), ())), preferred_element_type=F32)


def dot_nn(a, b):
    return lax.dot_general(a, b, (((1,), (0,)), ((), ())), preferred_element_type=F32)


class Attention:
    def __init__(self, docs_ref, q_ref, kv_ref, g_ref, keep_ref, out_ref, dq_ref, dkv_ref, scratch):
        (self.s, self.w, self.qs, self.qt, self.gs, self.gt, self.acc, self.mx, self.st, self.inv,
         self.dkt, self.dvt) = scratch
        self.docs, self.q, self.kv, self.g, self.keep = docs_ref, q_ref, kv_ref, g_ref, keep_ref
        self.out, self.dq, self.dkv = out_ref, dq_ref, dkv_ref
        self.first = 2 * lax.axis_index("ctx") - 16

    def part(self, r, j, left):
        cols = slice(0, E) if left else slice(E, 2 * E)
        if r == 1:
            return self.kv[j + 1, :, cols]
        return jnp.concatenate([self.kv[j, BLK:2 * BLK, cols], self.kv[j + 1, 0:BLK, cols]], axis=0)

    def columns(self, r, j):
        return pl.ds(pl.multiple_of((1 + r) * BLK + j * 2 * BLK, BLK), 2 * BLK)

    def forward(self, r):
        expo = math.log2(math.e) / math.sqrt(E)
        scale = 1.0 / 0.9
        lane = lax.broadcasted_iota(jnp.int32, (BLK, BLK), 1)
        row = lax.broadcasted_iota(jnp.int32, (BLK, BLK), 0)
        causal = jnp.where(lane <= row, 0.0, -jnp.inf).astype(F32)
        lane2 = lax.broadcasted_iota(jnp.int32, (1, 2 * BLK), 1)
        document = self.docs[self.first + 16 + r]
        low = 16 + r
        for w in range(1 + r, 16 + r):
            there = jnp.maximum(self.first + w, 0)
            same = jnp.where(self.docs[there] == document, 1, 0)
            low = low - jnp.where(self.first + w >= 0, same, 0)
        rows = pl.ds(r * BLK, BLK)
        for h in range(GROUP):
            part = self.q[rows, pl.ds(h * E, E)]
            self.qs[r, pl.ds(h * BLK, BLK), :] = part
            self.qt[r, :, pl.ds(h * BLK, BLK)] = part.T
        self.mx[...] = jnp.full_like(self.mx, -jnp.inf)

        def score_step(j, extra):
            s = dot_nt(self.qs[r], self.part(r, j, True))
            block = (1 + r) + 2 * j + lane2 // BLK
            bias = jnp.where(block >= low, 0.0, -jnp.inf).astype(F32)
            for h in range(GROUP):
                part = s[h * BLK:(h + 1) * BLK] + bias
                left, right = part[:, :BLK], part[:, BLK:]
                if extra:
                    right = right + causal
                hr = pl.ds(h * BLK, BLK)
                self.s[r, j, hr, 0:BLK] = left
                self.s[r, j, hr, BLK:2 * BLK] = right
                self.mx[hr, :] = jnp.maximum(self.mx[hr, :], jnp.maximum(left, right))

        def score_body(j, c):
            score_step(j, False)
            return c
        lax.fori_loop(0, PAIRS - 1, score_body, 0)
        score_step(PAIRS - 1, True)

        for h in range(GROUP):
            hr = pl.ds(h * BLK, BLK)
            top = jnp.max(self.mx[hr, :], axis=1, keepdims=True)
            self.st[hr, :] = jnp.broadcast_to(top, (BLK, BLK))
        self.mx[...] = jnp.zeros_like(self.mx)
        self.acc[...] = jnp.zeros_like(self.acc)

        def out_body(j, c):
            kb = self.table_row(r, j)
            for h in range(GROUP):
                hr = pl.ds(h * BLK, BLK)
                top = self.st[hr, :]
                left = jnp.exp2((self.s[r, j, hr, 0:BLK] - top) * expo)
                right = jnp.exp2((self.s[r, j, hr, BLK:2 * BLK] - top) * expo)
                self.s[r, j, hr, 0:BLK] = left
                self.s[r, j, hr, BLK:2 * BLK] = right
                self.mx[hr, :] = self.mx[hr, :] + (left + right)
                self.w[r, j, hr, 0:BLK] = (left * self.keep[h, pl.ds(kb, BLK), :]).astype(BF16)
                self.w[r, j, hr, BLK:2 * BLK] = (right * self.keep[h, pl.ds(kb + 1, BLK), :]).astype(BF16)
            self.acc[...] += dot_nn(self.w[r, j], self.part(r, j, False))
            return c
        lax.fori_loop(0, PAIRS, out_body, 0)

        for h in range(GROUP):
            hr = pl.ds(h * BLK, BLK)
            total = jnp.sum(self.mx[hr, :], axis=1, keepdims=True)
            inverse = 1.0 / total
            self.out[rows, pl.ds(h * E, E)] = (self.acc[hr, :] * (inverse * scale)).astype(BF16)
            self.inv[r, hr, :] = jnp.broadcast_to(inverse, (BLK, BLK))

    def table_row(self, r, j):
        kb = self.first + (1 + r) + 2 * j
        return jnp.where(kb < 0, BLK - 1, kb)

    def prepare(self, r):
        scale = 1.0 / 0.9
        rows = pl.ds(r * BLK, BLK)
        for h in range(GROUP):
            hr = pl.ds(h * BLK, BLK)
            cols = pl.ds(h * E, E)
            inverse = self.inv[r, hr, :]
            grad = self.g[rows, cols].astype(F32)
            delta = jnp.sum(grad * self.out[rows, cols].astype(F32), axis=1, keepdims=True)
            self.st[hr, :] = delta * inverse
            scaled = (grad * (inverse * scale)).astype(BF16)
            self.gs[hr, :] = scaled
            self.gt[:, hr] = scaled.T
        self.acc[...] = jnp.zeros_like(self.acc)

    def backward(self, r, begin, end):
        def grad_body(j, c):
            kb = self.table_row(r, j)
            dw = dot_nt(self.gs[...], self.part(r, j, False))
            self.dvt[:, self.columns(r, j)] += dot_nn(self.gt[...], self.w[r, j])
            for h in range(GROUP):
                hr = pl.ds(h * BLK, BLK)
                delta = self.st[hr, :]
                part = dw[h * BLK:(h + 1) * BLK]
                left = self.s[r, j, hr, 0:BLK] * (part[:, :BLK] * self.keep[h, pl.ds(kb, BLK), :] - delta)
                right = self.s[r, j, hr, BLK:2 * BLK] * (
                    part[:, BLK:] * self.keep[h, pl.ds(kb + 1, BLK), :] - delta)
                self.w[r, j, hr, 0:BLK] = left.astype(BF16)
                self.w[r, j, hr, BLK:2 * BLK] = right.astype(BF16)
            self.acc[...] += dot_nn(self.w[r, j], self.part(r, j, True))
            self.dkt[:, self.columns(r, j)] += dot_nn(self.qt[r], self.w[r, j])
            return c
        lax.fori_loop(begin, end, grad_body, 0)

    def store_query_grad(self, r):
        for h in range(GROUP):
            hr = pl.ds(h * BLK, BLK)
            self.dq[pl.ds(r * BLK, BLK), pl.ds(h * E, E)] = (self.acc[hr, :] * (1.0 / math.sqrt(E))).astype(BF16)

    def store_slot(self, slot):
        cs = pl.ds(slot * 2 * BLK, 2 * BLK)
        self.dkv[slot, :, 0:E] = (self.dkt[:, cs] * (1.0 / math.sqrt(E))).T.astype(BF16)
        self.dkv[slot, :, E:2 * E] = self.dvt[:, cs].T.astype(BF16)


def attn_scratch():
    rows = GROUP * BLK
    return [pltpu.VMEM((2, PAIRS, rows, 2 * BLK), F32),
            pltpu.VMEM((2, PAIRS, rows, 2 * BLK), BF16),
            pltpu.VMEM((2, rows, E), BF16),
            pltpu.VMEM((2, E, rows), BF16),
            pltpu.VMEM((rows, E), BF16),
            pltpu.VMEM((E, rows), BF16),
            pltpu.VMEM((rows, E), F32),
            pltpu.VMEM((rows, BLK), F32),
            pltpu.VMEM((rows, BLK), F32),
            pltpu.VMEM((2, rows, BLK), F32),
            pltpu.VMEM((E, WIN), F32),
            pltpu.VMEM((E, WIN), F32)]


def whole_kernel(docs_ref, mask_ref, table_ref, q_ref, k_ref, v_ref, g_ref, bits_ref,
                 ob_ref, gq_ref, gk_ref, gv_ref,
                 qb_ref, win_ref, gb_ref, keep_ref, out_ref, dq_ref, dkv_ref,
                 r_ref, zs_ref, zr_ref, own_ref, fin_ref,
                 kv_send, kv_recv, q_send, q_recv, z_send, z_recv, y_send, y_recv, own_sem,
                 dkv_send, dkv_recv, dq_send, dq_recv, dz_send, dz_recv, dy_send, dy_recv, down_sem,
                 *scratch):
    zi, yi, head = place()
    ctx = zi * NY + yi
    spot = (zi, yi, head)
    grad_move = Relay(mask_ref, table_ref, g_ref, gb_ref, scratch[:RELAY_REFS], spot)
    out_move = Relay(mask_ref, table_ref, out_ref, ob_ref, scratch[RELAY_REFS:2 * RELAY_REFS], spot)
    attn = Attention(docs_ref, qb_ref, win_ref, gb_ref, keep_ref, out_ref, dq_ref, dkv_ref,
                     scratch[2 * RELAY_REFS:])
    mine = pl.ds(pl.multiple_of(head * 32, 32), 32)
    wide = pl.ds(pl.multiple_of(head * GROUP * E, GROUP * E), GROUP * E)
    slim = pl.ds(pl.multiple_of(head * E, E), E)
    greet(zi, yi, head)

    own = [
        pltpu.make_async_copy(k_ref.at[:, slim], win_ref.at[8, mine, pl.ds(0, E)], own_sem.at[0]),
        pltpu.make_async_copy(v_ref.at[:, slim], win_ref.at[8, mine, pl.ds(E, E)], own_sem.at[1]),
        pltpu.make_async_copy(q_ref.at[:, wide], qb_ref.at[mine, :], own_sem.at[2]),
    ]
    for copy in own:
        copy.start()
    kv_copies = []
    for d in range(1, NH):
        to = (head + d) % NH
        cols = pl.ds(pl.multiple_of(to * E, E), E)
        for part, ref in enumerate((k_ref, v_ref)):
            copy = remote(ref.at[:, cols], win_ref.at[8, mine, pl.ds(part * E, E)],
                          kv_send.at[part, d], kv_recv.at[part, d], ctx, to)
            copy.start()
            kv_copies.append(copy)
    q_copies = []
    for d in range(1, NH):
        to = (head + d) % NH
        cols = pl.ds(pl.multiple_of(to * GROUP * E, GROUP * E), GROUP * E)
        copy = remote(q_ref.at[:, cols], qb_ref.at[mine, :], q_send.at[d], q_recv.at[d], ctx, to)
        copy.start()
        q_copies.append(copy)
    grad_move.step(0)
    build_keep(bits_ref, keep_ref)
    attn.dkt[...] = jnp.zeros_like(attn.dkt)
    attn.dvt[...] = jnp.zeros_like(attn.dvt)
    own[0].wait()
    own[1].wait()
    for copy in kv_copies:
        copy.wait_recv()
    z_copies = []
    for d in (1, 2):
        copy = remote(win_ref.at[8], win_ref.at[8 - 4 * d], z_send.at[d], z_recv.at[d],
                      ((zi + d) % NZ) * NY + yi, head)
        copy.start()
        z_copies.append(copy)
    y_copies = []
    for part in range(2):
        for k in range(1, NY):
            wrap = (yi + k) // NY
            y_copies.append((part, k, wrap, remote(
                win_ref.at[8 - 4 * part - 4 * wrap], win_ref.at[8 - 4 * part - k],
                y_send.at[part, k], y_recv.at[part, k], zi * NY + (yi + k) % NY, head)))
    for part, k, wrap, copy in y_copies:
        if part == 0:
            @pl.when(wrap == 0)
            def _(copy=copy):
                copy.start()
    z_copies[0].wait_recv()
    for part, k, wrap, copy in y_copies:
        @pl.when(wrap == 1 - part)
        def _(copy=copy):
            copy.start()
    grad_move.step(1)
    z_copies[1].wait_recv()
    for part, k, wrap, copy in y_copies:
        if part == 1:
            @pl.when(wrap == 1)
            def _(copy=copy):
                copy.start()
    grad_move.step(2)
    for copy in q_copies:
        copy.wait_recv()
    own[2].wait()
    for _, _, _, copy in y_copies:
        copy.wait_recv()

    grad_move.step(3)
    attn.forward(0)
    grad_move.step(4)
    attn.forward(1)
    grad_move.step(5)
    out_move.step(0)
    grad_move.finish()

    dq_copies = []

    def send_query_grads(r):
        for d in range(1, NH):
            to = (head + d) % NH
            rows = pl.ds(pl.multiple_of(to * 32, 32), 32)
            copy = remote(dq_ref.at[rows, :], gq_ref.at[:, wide], dq_send.at[d], dq_recv.at[d], ctx, to)
            if r == 0:
                dq_copies.append(copy)

            @pl.when(to // (NH // 2) == r)
            def _(copy=copy):
                copy.start()

    dy_copies = []

    def send_slots(part):
        for k in range(1, NY):
            slot = 8 - 4 * part - k
            attn.store_slot(slot)
            copy = remote(dkv_ref.at[slot], r_ref.at[part, k - 1],
                          dy_send.at[part, k], dy_recv.at[part, k], zi * NY + (yi + NY - k) % NY, head)
            copy.start()
            dy_copies.append(copy)

    attn.prepare(0)
    attn.backward(0, 0, PAIRS // 2)
    out_move.step(1)
    attn.backward(0, PAIRS // 2, PAIRS)
    attn.store_query_grad(0)
    send_query_grads(0)
    out_move.step(2)
    attn.prepare(1)
    attn.backward(1, 0, PAIRS // 2)
    send_slots(1)
    out_move.step(3)
    attn.backward(1, PAIRS // 2, PAIRS)
    send_slots(0)
    attn.store_query_grad(1)
    send_query_grads(1)
    for slot in (0, 4, 8):
        attn.store_slot(slot)
    down = [pltpu.make_async_copy(dq_ref.at[mine, :], gq_ref.at[:, wide], down_sem.at[0])]
    down[0].start()
    out_move.step(4)

    for copy in dy_copies:
        copy.wait_recv()
    sums = [dkv_ref[8 - 4 * p].astype(F32) for p in range(3)]
    for k in range(1, NY):
        wraps = (yi + k) // NY > 0
        first, second = r_ref[0, k - 1].astype(F32), r_ref[1, k - 1].astype(F32)
        zero = jnp.zeros_like(first)
        sums[0] = sums[0] + jnp.where(wraps, zero, first)
        sums[1] = sums[1] + jnp.where(wraps, first, second)
        sums[2] = sums[2] + jnp.where(wraps, second, zero)
    zs_ref[0] = sums[1].astype(BF16)
    zs_ref[1] = sums[2].astype(BF16)
    own_ref[...] = sums[0]
    dz_copies = []
    for d in (2, 1):
        copy = remote(zs_ref.at[d - 1], zr_ref.at[d - 1], dz_send.at[d], dz_recv.at[d],
                      ((zi + NZ - d) % NZ) * NY + yi, head)
        copy.start()
        dz_copies.append(copy)
    out_move.step(5)
    for copy in dz_copies:
        copy.wait_recv()
    fin_ref[...] = (own_ref[...] + zr_ref[0].astype(F32) + zr_ref[1].astype(F32)).astype(BF16)
    dkv_copies = []
    for d in range(1, NH):
        to = (head + d) % NH
        rows = pl.ds(pl.multiple_of(to * 32, 32), 32)
        for part, ref in enumerate((gk_ref, gv_ref)):
            copy = remote(fin_ref.at[rows, pl.ds(part * E, E)], ref.at[:, slim],
                          dkv_send.at[part, d], dkv_recv.at[part, d], ctx, to)
            copy.start()
            dkv_copies.append(copy)
    for part, ref in enumerate((gk_ref, gv_ref)):
        copy = pltpu.make_async_copy(fin_ref.at[mine, pl.ds(part * E, E)], ref.at[:, slim],
                                     down_sem.at[1 + part])
        copy.start()
        down.append(copy)
    out_move.finish()
    for copy in dq_copies + dkv_copies:
        copy.wait_recv()
    for copy in down:
        copy.wait()
    grad_move.drain()
    out_move.drain()
    for copy in kv_copies + q_copies + z_copies + dq_copies + dkv_copies + dy_copies + dz_copies:
        copy.wait_send()
    for _, _, _, copy in y_copies:
        copy.wait_send()


def on_device(query, key, value, grad_out, doc_ids, relay_mask, drop_bits):
    vm = pl.BlockSpec(memory_space=pltpu.VMEM)
    sm = pl.BlockSpec(memory_space=pltpu.SMEM)
    dma = pltpu.SemaphoreType.DMA
    links = [dma((2, NH)), dma((2, NH)), dma((NH,)), dma((NH,)), dma((3,)), dma((3,)),
             dma((2, NY)), dma((2, NY)), dma((3,))]
    return pl.pallas_call(
        whole_kernel,
        out_shape=(jax.ShapeDtypeStruct((2 * BLK, GROUP * E), BF16),
                   jax.ShapeDtypeStruct((32, NH * GROUP * E), BF16),
                   jax.ShapeDtypeStruct((32, NH * E), BF16),
                   jax.ShapeDtypeStruct((32, NH * E), BF16)),
        in_specs=[sm, sm, sm, vm, vm, vm, vm, vm],
        out_specs=(vm, vm, vm, vm),
        scratch_shapes=[
            pltpu.VMEM((2 * BLK, GROUP * E), BF16),
            pltpu.VMEM((9, 2 * BLK, 2 * E), BF16),
            pltpu.VMEM((2 * BLK, GROUP * E), BF16),
            pltpu.VMEM((GROUP, 2 * BLK, BLK), F32),
            pltpu.VMEM((2 * BLK, GROUP * E), BF16),
            pltpu.VMEM((2 * BLK, GROUP * E), BF16),
            pltpu.VMEM((9, 2 * BLK, 2 * E), BF16),
            pltpu.VMEM((2, NY - 1, 2 * BLK, 2 * E), BF16),
            pltpu.VMEM((2, 2 * BLK, 2 * E), BF16),
            pltpu.VMEM((2, 2 * BLK, 2 * E), BF16),
            pltpu.VMEM((2 * BLK, 2 * E), F32),
            pltpu.VMEM((2 * BLK, 2 * E), BF16),
        ] + links + links + relay_scratch() + relay_scratch() + attn_scratch(),
        compiler_params=pltpu.CompilerParams(
            collective_id=0, has_side_effects=True, vmem_limit_bytes=60 * 1024 * 1024),
    )(doc_ids, relay_mask, route_table(), query, key, value, grad_out, drop_bits.transpose(0, 2, 1))


def solution(mesh):
    placed = (
        P(("ctx", "head"), None),
        P(("ctx", "head"), None),
        P(("ctx", "head"), None),
        P("ctx", "head"),
        P(),
        P(),
        P("head", None, None),
    )
    return jax.shard_map(
        on_device,
        mesh=mesh,
        in_specs=placed,
        out_specs=(
            P("ctx", "head"),
            P(("ctx", "head"), None),
            P(("ctx", "head"), None),
            P(("ctx", "head"), None),
        ),
        check_vma=False,
    )
```

time: 139 us -> 106 us (0.76)
  the two profiles are of different devices: /device:TPU:6 before, /device:TPU:1 now
where the time goes in v1:
time: 106 us
  Pallas kernels  101 us (95%)
  local copies, waits for them, and re-layouts  4.28 us (4%)
    pallas_call x1, Pallas kernels, on_device(): pl.pallas_call(whole_kernel, out_shape=(jax.ShapeDtypeStruct((2 * BLK, GR...  101 us
    unnamed x10, local copies, waits for them, and re-layouts  4.28 us

profile of v1, /device:TPU:1, one launch (start us, length us, event | category | flops | bytes accessed | tf_op | source)
XLA Modules:
  0.0 105.8 jit_solution(9032523715255869955)
XLA Ops:
  0.6 100.9 %shard_map.111 = (bf16[256,1024]{1,0:T(8,128)(2,1)}, bf16[32,8192]{1,0:T(8,128)(2,1)}, bf16[32,1024]{1,0:T(8,128)(2,1)}, bf16[32,1024]{1,0:T(8,128)(2,1)}) custom-call(s32[64]{0:T(128)} %docs_ref.1, s32[2]{0:T(128)} %mask_ref.1, s32[736]{0:T(1024)} %constant.2.clone.table_ref, bf16[32,8192]{1,0:T(8,128)(2,1)} %q_ref.1, bf16[32,1024]{1,0:T(8,128)(2,1)} %k_ref.1, ...), custom_call_target="tpu_custom_call" | custom-call | tf_op jit(solution)/shard_map/pallas_call | solution.py:558
  101.5 0.0 copy-start
  101.5 1.9 %copy.16 = bf16[256,1024]{1,0:T(8,128)(2,1)} copy(bf16[256,1024]{1,0:T(8,128)(2,1)} %get-tuple-element.8) | data formatting | bytes 1048576
  103.4 0.0 copy-done
  103.4 0.0 copy-start.2
  103.5 0.8 copy.17
  104.2 0.1 copy-done.2
  104.3 0.0 copy-start.1
  104.3 0.6 copy.18
  104.9 0.2 copy-done.1
  105.2 0.6 copy.19
Async XLA Ops:
  101.5 1.9 %copy-start = (bf16[32,8192]{1,0:T(8,128)(2,1)S(1)}, bf16[32,8192]{1,0:T(8,128)(2,1)}, u32[]{:S(2)}) copy-start(bf16[32,8192]{1,0:T(8,128)(2,1)} %get-tuple-element.9) | copy-start | bytes 1572868
  103.4 0.9 copy-start.2
  104.3 0.9 copy-start.1

commit v2 on v1

--- a/solution.py
+++ b/solution.py
@@ -158,8 +158,10 @@
             else:
                 self.dst[self.region(n, piece)] = chosen
 
-    def step(self, k):
+    def step(self, r, k):
         for n in range(len(STREAMS)):
+            if STREAMS[n][0] != r:
+                continue
             which, t = self.plan[n][k]
             ring = self.rings[n][which]
             if t > 0:
@@ -177,9 +179,10 @@
                 ring["last"].append(copy)
                 self.copies.append(copy)
 
-    def finish(self):
+    def finish(self, r):
         for n in range(len(STREAMS)):
-            self.close(n, 1)
+            if STREAMS[n][0] == r:
+                self.close(n, 1)
 
     def drain(self):
         for copy in self.copies:
@@ -207,25 +210,32 @@
 
 
 class Attention:
-    def __init__(self, docs_ref, q_ref, kv_ref, g_ref, keep_ref, out_ref, dq_ref, dkv_ref, scratch):
+    def __init__(self, docs_ref, q_ref, kw_ref, vw_ref, g_ref, keep_ref, out_ref, dq_ref, dkv_ref, scratch):
         (self.s, self.w, self.qs, self.qt, self.gs, self.gt, self.acc, self.mx, self.st, self.inv,
          self.dkt, self.dvt) = scratch
-        self.docs, self.q, self.kv, self.g, self.keep = docs_ref, q_ref, kv_ref, g_ref, keep_ref
+        self.docs, self.q, self.g, self.keep = docs_ref, q_ref, g_ref, keep_ref
+        self.kw, self.vw = kw_ref, vw_ref
         self.out, self.dq, self.dkv = out_ref, dq_ref, dkv_ref
         self.first = 2 * lax.axis_index("ctx") - 16
 
     def part(self, r, j, left):
-        cols = slice(0, E) if left else slice(E, 2 * E)
+        ref = self.kw if left else self.vw
         if r == 1:
-            return self.kv[j + 1, :, cols]
-        return jnp.concatenate([self.kv[j, BLK:2 * BLK, cols], self.kv[j + 1, 0:BLK, cols]], axis=0)
+            return ref[j + 1]
+        return jnp.concatenate([ref[j, BLK:2 * BLK, :], ref[j + 1, 0:BLK, :]], axis=0)
 
     def columns(self, r, j):
         return pl.ds(pl.multiple_of((1 + r) * BLK + j * 2 * BLK, BLK), 2 * BLK)
 
-    def forward(self, r):
-        expo = math.log2(math.e) / math.sqrt(E)
-        scale = 1.0 / 0.9
+    def setup(self, r):
+        rows = pl.ds(r * BLK, BLK)
+        for h in range(GROUP):
+            part = self.q[rows, pl.ds(h * E, E)]
+            self.qs[r, pl.ds(h * BLK, BLK), :] = part
+            self.qt[r, :, pl.ds(h * BLK, BLK)] = part.T
+        self.mx[r] = jnp.full_like(self.mx[r], -jnp.inf)
+
+    def scores(self, r, begin, end):
         lane = lax.broadcasted_iota(jnp.int32, (BLK, BLK), 1)
         row = lax.broadcasted_iota(jnp.int32, (BLK, BLK), 0)
         causal = jnp.where(lane <= row, 0.0, -jnp.inf).astype(F32)
@@ -236,12 +246,6 @@
             there = jnp.maximum(self.first + w, 0)
             same = jnp.where(self.docs[there] == document, 1, 0)
             low = low - jnp.where(self.first + w >= 0, same, 0)
-        rows = pl.ds(r * BLK, BLK)
-        for h in range(GROUP):
-            part = self.q[rows, pl.ds(h * E, E)]
-            self.qs[r, pl.ds(h * BLK, BLK), :] = part
-            self.qt[r, :, pl.ds(h * BLK, BLK)] = part.T
-        self.mx[...] = jnp.full_like(self.mx, -jnp.inf)
 
         def score_step(j, extra):
             s = dot_nt(self.qs[r], self.part(r, j, True))
@@ -255,19 +259,24 @@
                 hr = pl.ds(h * BLK, BLK)
                 self.s[r, j, hr, 0:BLK] = left
                 self.s[r, j, hr, BLK:2 * BLK] = right
-                self.mx[hr, :] = jnp.maximum(self.mx[hr, :], jnp.maximum(left, right))
+                self.mx[r, hr, :] = jnp.maximum(self.mx[r, hr, :], jnp.maximum(left, right))
 
         def score_body(j, c):
             score_step(j, False)
             return c
-        lax.fori_loop(0, PAIRS - 1, score_body, 0)
-        score_step(PAIRS - 1, True)
-
+        lax.fori_loop(begin, min(end, PAIRS - 1), score_body, 0)
+        if end == PAIRS:
+            score_step(PAIRS - 1, True)
+
+    def weigh(self, r):
+        expo = math.log2(math.e) / math.sqrt(E)
+        scale = 1.0 / 0.9
+        rows = pl.ds(r * BLK, BLK)
         for h in range(GROUP):
             hr = pl.ds(h * BLK, BLK)
-            top = jnp.max(self.mx[hr, :], axis=1, keepdims=True)
+            top = jnp.max(self.mx[r, hr, :], axis=1, keepdims=True)
             self.st[hr, :] = jnp.broadcast_to(top, (BLK, BLK))
-        self.mx[...] = jnp.zeros_like(self.mx)
+        self.mx[r] = jnp.zeros_like(self.mx[r])
         self.acc[...] = jnp.zeros_like(self.acc)
 
         def out_body(j, c):
@@ -279,7 +288,7 @@
                 right = jnp.exp2((self.s[r, j, hr, BLK:2 * BLK] - top) * expo)
                 self.s[r, j, hr, 0:BLK] = left
                 self.s[r, j, hr, BLK:2 * BLK] = right
-                self.mx[hr, :] = self.mx[hr, :] + (left + right)
+                self.mx[r, hr, :] = self.mx[r, hr, :] + (left + right)
                 self.w[r, j, hr, 0:BLK] = (left * self.keep[h, pl.ds(kb, BLK), :]).astype(BF16)
                 self.w[r, j, hr, BLK:2 * BLK] = (right * self.keep[h, pl.ds(kb + 1, BLK), :]).astype(BF16)
             self.acc[...] += dot_nn(self.w[r, j], self.part(r, j, False))
@@ -288,7 +297,7 @@
 
         for h in range(GROUP):
             hr = pl.ds(h * BLK, BLK)
-            total = jnp.sum(self.mx[hr, :], axis=1, keepdims=True)
+            total = jnp.sum(self.mx[r, hr, :], axis=1, keepdims=True)
             inverse = 1.0 / total
             self.out[rows, pl.ds(h * E, E)] = (self.acc[hr, :] * (inverse * scale)).astype(BF16)
             self.inv[r, hr, :] = jnp.broadcast_to(inverse, (BLK, BLK))
@@ -351,7 +360,7 @@
             pltpu.VMEM((rows, E), BF16),
             pltpu.VMEM((E, rows), BF16),
             pltpu.VMEM((rows, E), F32),
-            pltpu.VMEM((rows, BLK), F32),
+            pltpu.VMEM((2, rows, BLK), F32),
             pltpu.VMEM((rows, BLK), F32),
             pltpu.VMEM((2, rows, BLK), F32),
             pltpu.VMEM((E, WIN), F32),
@@ -360,7 +369,7 @@
 
 def whole_kernel(docs_ref, mask_ref, table_ref, q_ref, k_ref, v_ref, g_ref, bits_ref,
                  ob_ref, gq_ref, gk_ref, gv_ref,
-                 qb_ref, win_ref, gb_ref, keep_ref, out_ref, dq_ref, dkv_ref,
+                 qb_ref, kw_ref, vw_ref, gb_ref, keep_ref, out_ref, dq_ref, dkv_ref,
                  r_ref, zs_ref, zr_ref, own_ref, fin_ref,
                  kv_send, kv_recv, q_send, q_recv, z_send, z_recv, y_send, y_recv, own_sem,
                  dkv_send, dkv_recv, dq_send, dq_recv, dz_send, dz_recv, dy_send, dy_recv, down_sem,
@@ -370,7 +379,7 @@
     spot = (zi, yi, head)
     grad_move = Relay(mask_ref, table_ref, g_ref, gb_ref, scratch[:RELAY_REFS], spot)
     out_move = Relay(mask_ref, table_ref, out_ref, ob_ref, scratch[RELAY_REFS:2 * RELAY_REFS], spot)
-    attn = Attention(docs_ref, qb_ref, win_ref, gb_ref, keep_ref, out_ref, dq_ref, dkv_ref,
+    attn = Attention(docs_ref, qb_ref, kw_ref, vw_ref, gb_ref, keep_ref, out_ref, dq_ref, dkv_ref,
                      scratch[2 * RELAY_REFS:])
     mine = pl.ds(pl.multiple_of(head * 32, 32), 32)
     wide = pl.ds(pl.multiple_of(head * GROUP * E, GROUP * E), GROUP * E)
@@ -378,21 +387,22 @@
     greet(zi, yi, head)
 
     own = [
-        pltpu.make_async_copy(k_ref.at[:, slim], win_ref.at[8, mine, pl.ds(0, E)], own_sem.at[0]),
-        pltpu.make_async_copy(v_ref.at[:, slim], win_ref.at[8, mine, pl.ds(E, E)], own_sem.at[1]),
+        pltpu.make_async_copy(k_ref.at[:, slim], kw_ref.at[8, mine, :], own_sem.at[0]),
+        pltpu.make_async_copy(v_ref.at[:, slim], vw_ref.at[8, mine, :], own_sem.at[1]),
         pltpu.make_async_copy(q_ref.at[:, wide], qb_ref.at[mine, :], own_sem.at[2]),
     ]
     for copy in own:
         copy.start()
-    kv_copies = []
-    for d in range(1, NH):
-        to = (head + d) % NH
-        cols = pl.ds(pl.multiple_of(to * E, E), E)
-        for part, ref in enumerate((k_ref, v_ref)):
-            copy = remote(ref.at[:, cols], win_ref.at[8, mine, pl.ds(part * E, E)],
-                          kv_send.at[part, d], kv_recv.at[part, d], ctx, to)
+    windows = (kw_ref, vw_ref)
+    kv_copies = [[], []]
+    for kind, ref in enumerate((k_ref, v_ref)):
+        for d in range(1, NH):
+            to = (head + d) % NH
+            cols = pl.ds(pl.multiple_of(to * E, E), E)
+            copy = remote(ref.at[:, cols], windows[kind].at[8, mine, :],
+                          kv_send.at[kind, d], kv_recv.at[kind, d], ctx, to)
             copy.start()
-            kv_copies.append(copy)
+            kv_copies[kind].append(copy)
     q_copies = []
     for d in range(1, NH):
         to = (head + d) % NH
@@ -400,58 +410,76 @@
         copy = remote(q_ref.at[:, cols], qb_ref.at[mine, :], q_send.at[d], q_recv.at[d], ctx, to)
         copy.start()
         q_copies.append(copy)
-    grad_move.step(0)
+    grad_move.step(0, 0)
+    grad_move.step(1, 0)
     build_keep(bits_ref, keep_ref)
     attn.dkt[...] = jnp.zeros_like(attn.dkt)
     attn.dvt[...] = jnp.zeros_like(attn.dvt)
-    own[0].wait()
-    own[1].wait()
-    for copy in kv_copies:
-        copy.wait_recv()
-    z_copies = []
-    for d in (1, 2):
-        copy = remote(win_ref.at[8], win_ref.at[8 - 4 * d], z_send.at[d], z_recv.at[d],
-                      ((zi + d) % NZ) * NY + yi, head)
-        copy.start()
-        z_copies.append(copy)
-    y_copies = []
-    for part in range(2):
-        for k in range(1, NY):
-            wrap = (yi + k) // NY
-            y_copies.append((part, k, wrap, remote(
-                win_ref.at[8 - 4 * part - 4 * wrap], win_ref.at[8 - 4 * part - k],
-                y_send.at[part, k], y_recv.at[part, k], zi * NY + (yi + k) % NY, head)))
-    for part, k, wrap, copy in y_copies:
-        if part == 0:
-            @pl.when(wrap == 0)
+    z_copies = [[], []]
+    y_copies = [[], []]
+    for kind, win in enumerate(windows):
+        own[kind].wait()
+        for copy in kv_copies[kind]:
+            copy.wait_recv()
+        for d in (1, 2):
+            copy = remote(win.at[8], win.at[8 - 4 * d], z_send.at[kind, d], z_recv.at[kind, d],
+                          ((zi + d) % NZ) * NY + yi, head)
+            copy.start()
+            z_copies[kind].append(copy)
+        for part in range(2):
+            for k in range(1, NY):
+                wrap = (yi + k) // NY
+                y_copies[kind].append((part, wrap, remote(
+                    win.at[8 - 4 * part - 4 * wrap], win.at[8 - 4 * part - k],
+                    y_send.at[kind, part, k], y_recv.at[kind, part, k], zi * NY + (yi + k) % NY, head)))
+        for part, wrap, copy in y_copies[kind]:
+            if part == 0:
+                @pl.when(wrap == 0)
+                def _(copy=copy):
+                    copy.start()
+    grad_move.step(0, 1)
+    for kind in range(2):
+        z_copies[kind][0].wait_recv()
+        for part, wrap, copy in y_copies[kind]:
+            @pl.when(wrap == 1 - part)
             def _(copy=copy):
                 copy.start()
-    z_copies[0].wait_recv()
-    for part, k, wrap, copy in y_copies:
-        @pl.when(wrap == 1 - part)
-        def _(copy=copy):
-            copy.start()
-    grad_move.step(1)
-    z_copies[1].wait_recv()
-    for part, k, wrap, copy in y_copies:
-        if part == 1:
-            @pl.when(wrap == 1)
-            def _(copy=copy):
-                copy.start()
-    grad_move.step(2)
+        z_copies[kind][1].wait_recv()
+        for part, wrap, copy in y_copies[kind]:
+            if part == 1:
+                @pl.when(wrap == 1)
+                def _(copy=copy):
+                    copy.start()
+        grad_move.step(kind, 2 - kind)
+    grad_move.step(0, 3)
     for copy in q_copies:
         copy.wait_recv()
     own[2].wait()
-    for _, _, _, copy in y_copies:
+    attn.setup(0)
+    attn.setup(1)
+    for part, _, copy in y_copies[0]:
+        if part == 0:
+            copy.wait_recv()
+    attn.scores(0, PAIRS // 2, PAIRS)
+    attn.scores(1, PAIRS // 2, PAIRS)
+    grad_move.step(0, 4)
+    grad_move.step(1, 2)
+    for part, _, copy in y_copies[0]:
+        if part == 1:
+            copy.wait_recv()
+    attn.scores(0, 0, PAIRS // 2)
+    attn.scores(1, 0, PAIRS // 2)
+    grad_move.step(0, 5)
+    grad_move.step(1, 3)
+    for _, _, copy in y_copies[1]:
         copy.wait_recv()
-
-    grad_move.step(3)
-    attn.forward(0)
-    grad_move.step(4)
-    attn.forward(1)
-    grad_move.step(5)
-    out_move.step(0)
-    grad_move.finish()
+    attn.weigh(0)
+    out_move.step(0, 0)
+    grad_move.step(1, 4)
+    attn.weigh(1)
+    out_move.step(1, 0)
+    grad_move.step(1, 5)
+    grad_move.finish(0)
 
     dq_copies = []
 
@@ -479,46 +507,64 @@
             dy_copies.append(copy)
 
     attn.prepare(0)
-    attn.backward(0, 0, PAIRS // 2)
-    out_move.step(1)
-    attn.backward(0, PAIRS // 2, PAIRS)
+    attn.backward(0, 0, 3)
+    out_move.step(0, 1)
+    out_move.step(1, 1)
+    attn.backward(0, 3, 6)
+    out_move.step(0, 2)
+    grad_move.finish(1)
+    attn.backward(0, 6, PAIRS)
     attn.store_query_grad(0)
     send_query_grads(0)
-    out_move.step(2)
+    attn.store_slot(0)
+    out_move.step(1, 2)
     attn.prepare(1)
-    attn.backward(1, 0, PAIRS // 2)
+    attn.backward(1, 0, 3)
     send_slots(1)
-    out_move.step(3)
-    attn.backward(1, PAIRS // 2, PAIRS)
+    out_move.step(0, 3)
+    out_move.step(1, 3)
+    attn.backward(1, 3, 5)
+    out_move.step(0, 4)
+    attn.backward(1, 5, 7)
     send_slots(0)
-    attn.store_query_grad(1)
-    send_query_grads(1)
-    for slot in (0, 4, 8):
-        attn.store_slot(slot)
-    down = [pltpu.make_async_copy(dq_ref.at[mine, :], gq_ref.at[:, wide], down_sem.at[0])]
-    down[0].start()
-    out_move.step(4)
-
-    for copy in dy_copies:
+    for copy in dy_copies[:NY - 1]:
         copy.wait_recv()
-    sums = [dkv_ref[8 - 4 * p].astype(F32) for p in range(3)]
+    wraps = [(yi + k) // NY > 0 for k in range(NY)]
+    total = dkv_ref[0].astype(F32)
     for k in range(1, NY):
-        wraps = (yi + k) // NY > 0
-        first, second = r_ref[0, k - 1].astype(F32), r_ref[1, k - 1].astype(F32)
-        zero = jnp.zeros_like(first)
-        sums[0] = sums[0] + jnp.where(wraps, zero, first)
-        sums[1] = sums[1] + jnp.where(wraps, first, second)
-        sums[2] = sums[2] + jnp.where(wraps, second, zero)
-    zs_ref[0] = sums[1].astype(BF16)
-    zs_ref[1] = sums[2].astype(BF16)
-    own_ref[...] = sums[0]
+        second = r_ref[1, k - 1].astype(F32)
+        total = total + jnp.where(wraps[k], second, jnp.zeros_like(second))
+    zs_ref[1] = total.astype(BF16)
     dz_copies = []
-    for d in (2, 1):
+
+    def send_plane(d):
         copy = remote(zs_ref.at[d - 1], zr_ref.at[d - 1], dz_send.at[d], dz_recv.at[d],
                       ((zi + NZ - d) % NZ) * NY + yi, head)
         copy.start()
         dz_copies.append(copy)
-    out_move.step(5)
+
+    send_plane(2)
+    out_move.step(1, 4)
+    attn.backward(1, 7, 8)
+    attn.store_query_grad(1)
+    send_query_grads(1)
+    for slot in (4, 8):
+        attn.store_slot(slot)
+    down = [pltpu.make_async_copy(dq_ref.at[mine, :], gq_ref.at[:, wide], down_sem.at[0])]
+    down[0].start()
+    for copy in dy_copies[NY - 1:]:
+        copy.wait_recv()
+    total = dkv_ref[4].astype(F32)
+    keep_here = dkv_ref[8].astype(F32)
+    for k in range(1, NY):
+        first, second = r_ref[0, k - 1].astype(F32), r_ref[1, k - 1].astype(F32)
+        total = total + jnp.where(wraps[k], first, second)
+        keep_here = keep_here + jnp.where(wraps[k], jnp.zeros_like(first), first)
+    zs_ref[0] = total.astype(BF16)
+    own_ref[...] = keep_here
+    send_plane(1)
+    out_move.step(0, 5)
+    out_move.step(1, 5)
     for copy in dz_copies:
         copy.wait_recv()
     fin_ref[...] = (own_ref[...] + zr_ref[0].astype(F32) + zr_ref[1].astype(F32)).astype(BF16)
@@ -536,36 +582,48 @@
                                      down_sem.at[1 + part])
         copy.start()
         down.append(copy)
-    out_move.finish()
+    out_move.finish(0)
+    out_move.finish(1)
     for copy in dq_copies + dkv_copies:
         copy.wait_recv()
     for copy in down:
         copy.wait()
     grad_move.drain()
     out_move.drain()
-    for copy in kv_copies + q_copies + z_copies + dq_copies + dkv_copies + dy_copies + dz_copies:
+    for copy in q_copies + dq_copies + dkv_copies + dy_copies + dz_copies:
         copy.wait_send()
-    for _, _, _, copy in y_copies:
-        copy.wait_send()
+    for kind in range(2):
+        for copy in kv_copies[kind] + z_copies[kind]:
+            copy.wait_send()
+        for _, _, copy in y_copies[kind]:
+            copy.wait_send()
+
+
+def settle_kernel(*refs):
+    for src, dst in zip(refs[:4], refs[4:]):
+        dst[...] = src[...]
 
 
 def on_device(query, key, value, grad_out, doc_ids, relay_mask, drop_bits):
     vm = pl.BlockSpec(memory_space=pltpu.VMEM)
     sm = pl.BlockSpec(memory_space=pltpu.SMEM)
     dma = pltpu.SemaphoreType.DMA
-    links = [dma((2, NH)), dma((2, NH)), dma((NH,)), dma((NH,)), dma((3,)), dma((3,)),
-             dma((2, NY)), dma((2, NY)), dma((3,))]
-    return pl.pallas_call(
-        whole_kernel,
-        out_shape=(jax.ShapeDtypeStruct((2 * BLK, GROUP * E), BF16),
+    heads = [dma((2, NH)), dma((2, NH)), dma((NH,)), dma((NH,))]
+    up = heads + [dma((2, 3)), dma((2, 3)), dma((2, 2, NY)), dma((2, 2, NY)), dma((3,))]
+    down = heads + [dma((3,)), dma((3,)), dma((2, NY)), dma((2, NY)), dma((3,))]
+    shapes = (jax.ShapeDtypeStruct((2 * BLK, GROUP * E), BF16),
                    jax.ShapeDtypeStruct((32, NH * GROUP * E), BF16),
                    jax.ShapeDtypeStruct((32, NH * E), BF16),
-                   jax.ShapeDtypeStruct((32, NH * E), BF16)),
+                   jax.ShapeDtypeStruct((32, NH * E), BF16))
+    results = pl.pallas_call(
+        whole_kernel,
+        out_shape=shapes,
         in_specs=[sm, sm, sm, vm, vm, vm, vm, vm],
         out_specs=(vm, vm, vm, vm),
         scratch_shapes=[
             pltpu.VMEM((2 * BLK, GROUP * E), BF16),
-            pltpu.VMEM((9, 2 * BLK, 2 * E), BF16),
+            pltpu.VMEM((9, 2 * BLK, E), BF16),
+            pltpu.VMEM((9, 2 * BLK, E), BF16),
             pltpu.VMEM((2 * BLK, GROUP * E), BF16),
             pltpu.VMEM((GROUP, 2 * BLK, BLK), F32),
             pltpu.VMEM((2 * BLK, GROUP * E), BF16),
@@ -576,10 +634,12 @@
             pltpu.VMEM((2, 2 * BLK, 2 * E), BF16),
             pltpu.VMEM((2 * BLK, 2 * E), F32),
             pltpu.VMEM((2 * BLK, 2 * E), BF16),
-        ] + links + links + relay_scratch() + relay_scratch() + attn_scratch(),
+        ] + up + down + relay_scratch() + relay_scratch() + attn_scratch(),
         compiler_params=pltpu.CompilerParams(
             collective_id=0, has_side_effects=True, vmem_limit_bytes=60 * 1024 * 1024),
     )(doc_ids, relay_mask, route_table(), query, key, value, grad_out, drop_bits.transpose(0, 2, 1))
+    return pl.pallas_call(
+        settle_kernel, out_shape=shapes, in_specs=[vm] * 4, out_specs=(vm,) * 4)(*results)
 
 
 def solution(mesh):

time: 106 us -> 94.5 us (0.89)
  Pallas kernels: 101 us -> 93.7 us
  local copies, waits for them, and re-layouts: 4.28 us -> 0 us
    pallas_call x1 -> x2, Pallas kernels: 101 us -> 93.7 us  [the longest x1 91.5 us: on_device(): pl.pallas_call(whole_kernel, out_shape=shapes, in_specs=[sm, sm, sm, vm,...]
    unnamed x10 -> x0, local copies, waits for them, and re-layouts: 4.28 us -> none
where the time goes in v2:
time: 94.5 us; the launch traced here: 94.3 us
  Pallas kernels  93.7 us (99%)
    pallas_call x1, Pallas kernels, on_device(): pl.pallas_call(whole_kernel, out_shape=shapes, in_specs=[sm, sm, sm, vm,...  91.5 us
    pallas_call x1, Pallas kernels, on_device(): pl.pallas_call(settle_kernel, out_shape=shapes, in_specs=[vm] * 4, out_sp...  2.24 us

profile of v2, /device:TPU:1, one launch (start us, length us, event | category | flops | bytes accessed | tf_op | source)
XLA Modules:
  0.0 94.3 jit_solution(13545470379148106402)
XLA Ops:
  0.6 91.5 %shard_map.111 = (bf16[256,1024]{1,0:T(8,128)(2,1)}, bf16[32,8192]{1,0:T(8,128)(2,1)}, bf16[32,1024]{1,0:T(8,128)(2,1)}, bf16[32,1024]{1,0:T(8,128)(2,1)}) custom-call(s32[64]{0:T(128)} %docs_ref.1, s32[2]{0:T(128)} %mask_ref.1, s32[736]{0:T(1024)} %constant.2.clone.table_ref, bf16[32,8192]{1,0:T(8,128)(2,1)} %q_ref.1, bf16[32,1024]{1,0:T(8,128)(2,1)} %k_ref.1, ...), custom_call_target="tpu_custom_call" | custom-call | tf_op jit(solution)/shard_map/pallas_call | solution.py:618
  92.1 2.2 %shard_map.112 = (bf16[256,1024]{1,0:T(8,128)(2,1)}, bf16[32,8192]{1,0:T(8,128)(2,1)}, bf16[32,1024]{1,0:T(8,128)(2,1)}, bf16[32,1024]{1,0:T(8,128)(2,1)}) custom-call(bf16[256,1024]{1,0:T(8,128)(2,1)} %get-tuple-element.8.refs_0_, bf16[32,8192]{1,0:T(8,128)(2,1)} %get-tuple-element.9.refs_1_, bf16[32,1024]{1,0:T(8,128)(2,1)} %get-tuple-element.10.refs_2_, ...), custom_call_target="tpu_custom_call" | custom-call | tf_op jit(solution)/shard_map/pallas_call | solution.py:641

commit v3 on v2

--- a/solution.py
+++ b/solution.py
@@ -450,8 +450,8 @@
                 @pl.when(wrap == 1)
                 def _(copy=copy):
                     copy.start()
-        grad_move.step(kind, 2 - kind)
-    grad_move.step(0, 3)
+    grad_move.step(0, 2)
+    grad_move.step(1, 1)
     for copy in q_copies:
         copy.wait_recv()
     own[2].wait()
@@ -462,19 +462,20 @@
             copy.wait_recv()
     attn.scores(0, PAIRS // 2, PAIRS)
     attn.scores(1, PAIRS // 2, PAIRS)
-    grad_move.step(0, 4)
+    grad_move.step(0, 3)
     grad_move.step(1, 2)
     for part, _, copy in y_copies[0]:
         if part == 1:
             copy.wait_recv()
     attn.scores(0, 0, PAIRS // 2)
     attn.scores(1, 0, PAIRS // 2)
-    grad_move.step(0, 5)
+    grad_move.step(0, 4)
     grad_move.step(1, 3)
     for _, _, copy in y_copies[1]:
         copy.wait_recv()
     attn.weigh(0)
     out_move.step(0, 0)
+    grad_move.step(0, 5)
     grad_move.step(1, 4)
     attn.weigh(1)
     out_move.step(1, 0)

time: 94.5 us -> 91.7 us (0.970)
  Pallas kernels: 93.7 us -> 90.9 us
    pallas_call x1, Pallas kernels: 91.5 us -> 88.7 us  [on_device(): pl.pallas_call(whole_kernel, out_shape=shapes, in_specs=[sm, sm, sm, vm,...]
where the time goes in v3:
time: 91.7 us; the launch traced here: 91.6 us
  Pallas kernels  90.9 us (99%)
    pallas_call x1, Pallas kernels, on_device(): pl.pallas_call(whole_kernel, out_shape=shapes, in_specs=[sm, sm, sm, vm,...  88.7 us
    pallas_call x1, Pallas kernels, on_device(): pl.pallas_call(settle_kernel, out_shape=shapes, in_specs=[vm] * 4, out_sp...  2.24 us

profile of v3, /device:TPU:1, one launch (start us, length us, event | category | flops | bytes accessed | tf_op | source)
XLA Modules:
  0.0 91.6 jit_solution(17726742450683484381)
XLA Ops:
  0.6 88.7 %shard_map.111 = (bf16[256,1024]{1,0:T(8,128)(2,1)}, bf16[32,8192]{1,0:T(8,128)(2,1)}, bf16[32,1024]{1,0:T(8,128)(2,1)}, bf16[32,1024]{1,0:T(8,128)(2,1)}) custom-call(s32[64]{0:T(128)} %docs_ref.1, s32[2]{0:T(128)} %mask_ref.1, s32[736]{0:T(1024)} %constant.2.clone.table_ref, bf16[32,8192]{1,0:T(8,128)(2,1)} %q_ref.1, bf16[32,1024]{1,0:T(8,128)(2,1)} %k_ref.1, ...), custom_call_target="tpu_custom_call" | custom-call | tf_op jit(solution)/shard_map/pallas_call | solution.py:619
  89.3 2.2 %shard_map.112 = (bf16[256,1024]{1,0:T(8,128)(2,1)}, bf16[32,8192]{1,0:T(8,128)(2,1)}, bf16[32,1024]{1,0:T(8,128)(2,1)}, bf16[32,1024]{1,0:T(8,128)(2,1)}) custom-call(bf16[256,1024]{1,0:T(8,128)(2,1)} %get-tuple-element.8.refs_0_, bf16[32,8192]{1,0:T(8,128)(2,1)} %get-tuple-element.9.refs_1_, bf16[32,1024]{1,0:T(8,128)(2,1)} %get-tuple-element.10.refs_2_, ...), custom_call_target="tpu_custom_call" | custom-call | tf_op jit(solution)/shard_map/pallas_call | solution.py:642
